TPU v7x, 32 devices: a whole 2x2x4 slice. The times are simulated.
32 devices in a mesh: groups: 2 (over x), blk: 16 (over z, y, core).
Axes of the slice: x: 2, y: 2, z: 4, core: 2. Of those that a mesh axis runs over, the one named last changes fastest.
Arguments:
- frames: bfloat16 [256, 16384], P(('groups', 'blk')), parts along dimension 0
- basis: bfloat16 [256, 64], P(('groups', 'blk')), parts along dimension 0, may hold values from -6 to 6
- density: bfloat16 [256], P(('groups', 'blk')), parts along dimension 0, may hold values from 0.25 to 4
Outputs:
- residual_block: bfloat16 [256, 64], P(('groups', 'blk')), parts along dimension 0
- coefficients: float32 [128, 64], P('groups'), parts along dimension 0
There are 2 independent parts, one for each index of `groups`. A program takes and returns all parts, laid end to end along the dimension named above; each array names one. Nothing has to cross between parts.
All inputs are finite; a program needn't handle non-finite values.
Results may differ from a plain program's by a relative error of at most 0.0045.
Values may be sent and summed in bfloat16 or wider, within the bound.
No kernel may reach another device: no remote copies, remote signals or barrier semaphores. Data moves between devices by JAX's collectives and lax.ppermute only.
A program may use at most 64 MiB of HBM per device.

v0:
```python
import jax
import jax.numpy as jnp
from jax import lax
from jax.sharding import PartitionSpec as P


def pair_kernel(left, left_norms, right):
    right_norms = jnp.sum(jnp.square(right.astype(jnp.float32)), axis=1)
    inner_products = lax.dot_general(
        left, right, (((1,), (1,)), ((), ())), preferred_element_type=jnp.float32
    )
    squared_dist = left_norms[:, None] + right_norms[None, :] - 2.0 * inner_products
    return jnp.exp(-squared_dist / left.shape[1])


def shards(frames, basis, density):
    own_norms = jnp.sum(jnp.square(frames.astype(jnp.float32)), axis=1)
    row_count = frames.shape[0]
    blocks = lax.all_gather(frames, "blk", axis=0, tiled=True)
    vectors = lax.all_gather(basis, "blk", axis=0, tiled=True)
    weights_in = lax.all_gather(density, "blk", axis=0, tiled=True)
    kernel = pair_kernel(frames, own_norms, blocks)
    forward = (kernel * weights_in.astype(jnp.float32)[None, :]).astype(jnp.bfloat16)
    numer = jnp.dot(forward, vectors, preferred_element_type=jnp.float32)
    totals = jnp.sum(forward.astype(jnp.float32), axis=1)
    numer, totals = (numer, totals)
    applied = numer / totals[:, None]
    basis_f = basis.astype(jnp.float32)
    local_coef = lax.dot_general(
        basis_f,
        applied,
        (((0,), (0,)), ((), ())),
        precision=lax.Precision.HIGHEST,
        preferred_element_type=jnp.float32,
    )
    coefficients = lax.psum(local_coef, "blk")
    frame_total = row_count * lax.axis_size("blk")
    projection = jnp.dot(
        basis_f, coefficients, precision=lax.Precision.HIGHEST, preferred_element_type=jnp.float32
    )
    residual_block = (applied - projection / frame_total).astype(jnp.bfloat16)
    return (residual_block, coefficients)


def solution(mesh):
    placed = (P(("groups", "blk"), None), P(("groups", "blk"), None), P(("groups", "blk")))
    return jax.shard_map(
        shards,
        mesh=mesh,
        in_specs=placed,
        out_specs=(P(("groups", "blk"), None), P("groups", None)),
        check_vma=False,
    )
```

profile of v0, /device:TPU:0, one launch (start us, length us, event | category | flops | bytes accessed | tf_op | source)
XLA Modules:
  0.0 137.7 jit_solution(3754534518135585667)
XLA Ops:
  7.2 0.0 copy-start.1
  7.2 0.0 all-gather.2.cloned.1.call-start
  7.2 0.7 all-gather.2.cloned.1.call-update
  7.9 1.2 dynamic-slice
  9.8 0.9 dynamic-update-slice
  10.7 35.4 %all-reduce = bf16[128]{0:T(256)(128)(2,1)S(1)} all-reduce(bf16[128]{0:T(256)(128)(2,1)S(1)} %dynamic-update-slice), channel_id=1, replica_groups=mesh['groups'=2,'blk'=16] {'blk'}, use_global_device_ids=true, to_apply=%add | all-reduce | flops 128 | bytes 512
  46.1 17.6 %all_gather.11 = bf16[128,64]{1,0:T(8,128)(2,1)S(1)} all-gather(bf16[8,64]{1,0:T(8,128)(2,1)} %param.4), channel_id=1, replica_groups=mesh['groups'=2,'blk'=16] {'blk'}, dimensions={0}, use_global_device_ids=true | all-gather | bytes 17408 | tf_op jit(solution)/shard_map/all_gather | solution.py:20
  63.7 1.2 multiply_reduce_fusion.1
  64.9 0.0 all-gather.2.cloned.1.call-done
  64.9 0.0 copy-start
  64.9 0.0 copy-start.2
  64.9 3.2 %multiply_reduce_fusion = f32[128]{0:T(128)S(1)} fusion(bf16[128,16384]{1,0:T(8,128)(2,1)} %all-gather.2.cloned.1.call-done), kind=kLoop, calls=%fused_computation | loop fusion | flops 6291328 | bytes 4194816 | tf_op jit(solution)/shard_map/reduce_sum | solution.py:8
  68.2 0.0 copy-done.1
  68.2 0.2 copy-done
  68.4 1.3 convert_reduce_fusion
  69.7 0.1 convolution_divide_fusion
  69.8 0.0 copy-done.2
  69.8 0.2 convolution_bitcast_fusion
  70.0 59.3 %psum.7 = f32[64,64]{0,1:T(8,128)S(1)} all-reduce(f32[64,64]{0,1:T(8,128)S(1)} %convolution_bitcast_fusion), channel_id=1, replica_groups=mesh['groups'=2,'blk'=16] {'blk'}, use_global_device_ids=true, to_apply=%region_3.0 | all-reduce | flops 4096 | bytes 32768 | tf_op jit(solution)/shard_map/psum | solution.py:36
  129.4 0.7 fusion.8
  130.1 0.7 copy.5
  (2 shorter events, 0.0 us)
Async XLA Ops:
  7.2 61.0 %copy-start.1 = (bf16[8,16384]{1,0:T(8,128)(2,1)S(1)}, bf16[8,16384]{1,0:T(8,128)(2,1)}, u32[]{:S(2)}) copy-start(bf16[8,16384]{1,0:T(8,128)(2,1)} %param.3) | copy-start | bytes 786436
  7.2 57.7 %all-gather.2.cloned.1.call-start = ((), (), s32[]{:S(2)}) async-start(), calls=%async_computation | async-start | bytes 4456448 | tf_op jit(solution)/shard_map/all_gather | solution.py:19
  64.9 3.5 %copy-start = (bf16[128,16384]{1,0:T(8,128)(2,1)S(1)}, bf16[128,16384]{1,0:T(8,128)(2,1)}, u32[]{:S(2)}) copy-start(bf16[128,16384]{1,0:T(8,128)(2,1)} %all-gather.2.cloned.1.call-done) | copy-start | bytes 12582916
  64.9 4.9 %copy-start.2 = (bf16[8,64]{1,0:T(8,128)(2,1)S(1)}, bf16[8,64]{1,0:T(8,128)(2,1)}, u32[]{:S(2)}) copy-start(bf16[8,64]{1,0:T(8,128)(2,1)} %param.4) | copy-start | bytes 3076
Sparse Core Ops, SparseCore 0:
  10.2 53.5 all-gather.1
where the time goes:
time: 138 us
  blocking collectives  112 us (81%)
  between operations  14.7 us (11%)
  other arithmetic  4.43 us (3%)
  local copies, waits for them, and re-layouts  3.01 us (2%)
  matrix products  2.4 us (2%)
    psum x1, blocking collectives, shards(): coefficients = lax.psum(local_coef, 'blk')  59.3 us
    unnamed x1, blocking collectives  35.4 us
    all_gather x1, blocking collectives, shards(): vectors = lax.all_gather(basis, 'blk', axis=0, tiled=True)  17.6 us
    reduce_sum x1, other arithmetic, pair_kernel(): right_norms = jnp.sum(jnp.square(right.astype(jnp.float32)), axis=1)  3.23 us
    unnamed x10, local copies, waits for them, and re-layouts  3.01 us
  transfers between devices with their start and end apart: 1, of which 0 were waited for; matrix products, arithmetic and copies ran while one was open for 2% of the time, Pallas kernels for 0%

commit v1 on v0

--- a/solution.py
+++ b/solution.py
@@ -2,6 +2,32 @@
 import jax.numpy as jnp
 from jax import lax
 from jax.sharding import PartitionSpec as P
+
+
+def _do_roots(vector):
+    axis_name = "blk"
+    all_values, n_now, state_next = (
+        lax.axis_size(axis_name),
+        lax.axis_index(axis_name),
+        vector.shape[0],
+    )
+    line_up = [(nth, (nth + 1) % all_values) for nth in range(all_values)]
+    found = [(nth, (nth - 1) % all_values) for nth in range(all_values)]
+    even = jnp.zeros((*vector.shape[:0], all_values * state_next, *vector.shape[1:]), vector.dtype)
+    even = lax.dynamic_update_slice_in_dim(even, vector, n_now * state_next, axis=0)
+    long_array = outcome_arr = vector
+    top = all_values // 2
+    for hop_no in range(1, top + 1):
+        long_array = lax.ppermute(long_array, axis_name=axis_name, perm=line_up)
+        even = lax.dynamic_update_slice_in_dim(
+            even, long_array, (n_now - hop_no) % all_values * state_next, axis=0
+        )
+        if hop_no < all_values - top:
+            outcome_arr = lax.ppermute(outcome_arr, axis_name=axis_name, perm=found)
+            even = lax.dynamic_update_slice_in_dim(
+                even, outcome_arr, (n_now + hop_no) % all_values * state_next, axis=0
+            )
+    return even
 
 
 def pair_kernel(left, left_norms, right):
@@ -17,7 +43,7 @@
     own_norms = jnp.sum(jnp.square(frames.astype(jnp.float32)), axis=1)
     row_count = frames.shape[0]
     blocks = lax.all_gather(frames, "blk", axis=0, tiled=True)
-    vectors = lax.all_gather(basis, "blk", axis=0, tiled=True)
+    vectors = _do_roots(basis)
     weights_in = lax.all_gather(density, "blk", axis=0, tiled=True)
     kernel = pair_kernel(frames, own_norms, blocks)
     forward = (kernel * weights_in.astype(jnp.float32)[None, :]).astype(jnp.bfloat16)

time: 138 us -> 160 us (1.16)
  starting transfers between devices: 0.04 us -> 32.2 us
  blocking collectives: 112 us -> 88.2 us
  waiting for transfers between devices: 0.69 us -> 14.1 us
    ppermute x0 -> x15, starting transfers between devices: none -> 32.2 us  [the longest x7 31.6 us: _do_roots(): outcome_arr = lax.ppermute(outcome_arr, axis_name=axis_name, perm=found)]
    all_gather x1 -> x0, blocking collectives: 17.6 us -> none  [shards(): vectors = lax.all_gather(basis, 'blk', axis=0, tiled=True)]
    ppermute x0 -> x15, waiting for transfers between devices: none -> 13.4 us  [the longest x8 13.1 us: _do_roots(): long_array = lax.ppermute(long_array, axis_name=axis_name, perm=line_up)]
    unnamed x1, blocking collectives: 35.4 us -> 30.5 us
    psum x1, blocking collectives: 59.3 us -> 57.6 us  [shards(): coefficients = lax.psum(local_coef, 'blk')]
  transfers between devices with their start and end apart: 1 -> 16, of which waited for: 0 -> 7; matrix products, arithmetic and copies ran while one was open for 2% -> 3% of each run, Pallas kernels for 0% -> 0%
where the time goes in v1:
time: 160 us
  blocking collectives  88.2 us (55%)
  starting transfers between devices  32.2 us (20%)
  between operations  14.8 us (9%)
  waiting for transfers between devices  14.1 us (9%)
  other arithmetic  4.43 us (3%)
  local copies, waits for them, and re-layouts  3.83 us (2%)
  matrix products  2.4 us (2%)
    psum x1, blocking collectives, shards(): coefficients = lax.psum(local_coef, 'blk')  57.6 us
    ppermute x7, starting transfers between devices, _do_roots(): outcome_arr = lax.ppermute(outcome_arr, axis_name=axis_name, perm=found)  31.6 us
    unnamed x1, blocking collectives  30.5 us
    ppermute x8, waiting for transfers between devices, _do_roots(): long_array = lax.ppermute(long_array, axis_name=axis_name, perm=line_up)  13.1 us
    reduce_sum x1, other arithmetic, pair_kernel(): right_norms = jnp.sum(jnp.square(right.astype(jnp.float32)), axis=1)  3.23 us
  transfers between devices with their start and end apart: 16, of which 7 were waited for; matrix products, arithmetic and copies ran while one was open for 3% of the time, Pallas kernels for 0%

profile of v1, /device:TPU:0, one launch (start us, length us, event | category | flops | bytes accessed | tf_op | source)
XLA Modules:
  0.0 160.0 jit_solution(2041472999556250784)
XLA Ops:
  7.2 0.0 copy-start.1
  7.2 0.0 all-gather.2.cloned.1.call-start
  7.2 0.7 all-gather.2.cloned.1.call-update
  7.9 0.5 collective-permute-start
  8.4 5.1 %collective-permute-start.1 = (bf16[8,64]{1,0:T(8,128)(2,1)}, bf16[8,64]{1,0:T(8,128)(2,1)S(1)}, u32[]{:S(2)}, u32[]{:S(2)}) collective-permute-start(bf16[8,64]{1,0:T(8,128)(2,1)} %param.4), channel_id=1, source_target_pairs={{0,15},{1,0},{2,1},{3,2},{4,3},{5,4},{6,5},{7,6},{8,7},{9,8},{10,9... | collective-permute-start | bytes 3080 | tf_op jit(solution)/shard_map/ppermute | solution.py:26
  13.5 1.2 dynamic-slice
  15.4 0.7 constant_dynamic-update-slice_fusion.15
  16.1 1.2 multiply_reduce_fusion.1
  17.3 0.9 dynamic-update-slice
  18.1 30.5 %all-reduce = bf16[128]{0:T(256)(128)(2,1)S(1)} all-reduce(bf16[128]{0:T(256)(128)(2,1)S(1)} %dynamic-update-slice), channel_id=1, replica_groups=mesh['groups'=2,'blk'=16] {'blk'}, use_global_device_ids=true, to_apply=%add | all-reduce | flops 128 | bytes 512
  48.8 0.0 collective-permute-done
  48.8 0.1 collective-permute-start.2
  48.8 0.0 collective-permute-done.1
  48.8 4.4 %collective-permute-start.3 = (bf16[8,64]{1,0:T(8,128)(2,1)S(1)}, bf16[8,64]{1,0:T(8,128)(2,1)S(1)}, u32[]{:S(2)}, u32[]{:S(2)}) collective-permute-start(bf16[8,64]{1,0:T(8,128)(2,1)S(1)} %collective-permute-done.1), channel_id=1, source_target_pairs={{0,15},{1,0},{2,1},{3,2},{4,3},{5,4},{6,5},{7,6},{8,7},{9,8},{10,9... | collective-permute-start | bytes 3080 | tf_op jit(solution)/shard_map/ppermute | solution.py:26
  53.3 1.2 collective-permute-done.2
  54.5 0.0 collective-permute-start.4
  54.5 0.0 collective-permute-done.3
  54.6 4.5 %collective-permute-start.5 = (bf16[8,64]{1,0:T(8,128)(2,1)S(1)}, bf16[8,64]{1,0:T(8,128)(2,1)S(1)}, u32[]{:S(2)}, u32[]{:S(2)}) collective-permute-start(bf16[8,64]{1,0:T(8,128)(2,1)S(1)} %collective-permute-done.3), channel_id=1, source_target_pairs={{0,15},{1,0},{2,1},{3,2},{4,3},{5,4},{6,5},{7,6},{8,7},{9,8},{10,9... | collective-permute-start | bytes 3080 | tf_op jit(solution)/shard_map/ppermute | solution.py:26
  59.1 1.3 collective-permute-done.4
  60.4 0.0 collective-permute-start.6
  60.4 0.0 collective-permute-done.5
  60.4 4.4 %collective-permute-start.7 = (bf16[8,64]{1,0:T(8,128)(2,1)S(1)}, bf16[8,64]{1,0:T(8,128)(2,1)S(1)}, u32[]{:S(2)}, u32[]{:S(2)}) collective-permute-start(bf16[8,64]{1,0:T(8,128)(2,1)S(1)} %collective-permute-done.5), channel_id=1, source_target_pairs={{0,15},{1,0},{2,1},{3,2},{4,3},{5,4},{6,5},{7,6},{8,7},{9,8},{10,9... | collective-permute-start | bytes 3080 | tf_op jit(solution)/shard_map/ppermute | solution.py:26
  64.8 1.2 collective-permute-done.6
  66.1 0.0 collective-permute-start.8
  66.1 0.0 collective-permute-done.7
  66.1 4.4 %collective-permute-start.9 = (bf16[8,64]{1,0:T(8,128)(2,1)S(1)}, bf16[8,64]{1,0:T(8,128)(2,1)S(1)}, u32[]{:S(2)}, u32[]{:S(2)}) collective-permute-start(bf16[8,64]{1,0:T(8,128)(2,1)S(1)} %collective-permute-done.7), channel_id=1, source_target_pairs={{0,15},{1,0},{2,1},{3,2},{4,3},{5,4},{6,5},{7,6},{8,7},{9,8},{10,9... | collective-permute-start | bytes 3080 | tf_op jit(solution)/shard_map/ppermute | solution.py:26
  70.5 1.2 collective-permute-done.8
  71.8 0.0 collective-permute-start.10
  71.8 0.0 collective-permute-done.9
  71.8 4.4 %collective-permute-start.11 = (bf16[8,64]{1,0:T(8,128)(2,1)S(1)}, bf16[8,64]{1,0:T(8,128)(2,1)S(1)}, u32[]{:S(2)}, u32[]{:S(2)}) collective-permute-start(bf16[8,64]{1,0:T(8,128)(2,1)S(1)} %collective-permute-done.9), channel_id=1, source_target_pairs={{0,15},{1,0},{2,1},{3,2},{4,3},{5,4},{6,5},{7,6},{8,7},{9,8},{10,9... | collective-permute-start | bytes 3080 | tf_op jit(solution)/shard_map/ppermute | solution.py:26
  76.2 1.2 collective-permute-done.10
  77.5 0.0 collective-permute-start.12
  77.5 0.0 collective-permute-done.11
  77.5 4.4 %collective-permute-start.13 = (bf16[8,64]{1,0:T(8,128)(2,1)S(1)}, bf16[8,64]{1,0:T(8,128)(2,1)S(1)}, u32[]{:S(2)}, u32[]{:S(2)}) collective-permute-start(bf16[8,64]{1,0:T(8,128)(2,1)S(1)} %collective-permute-done.11), channel_id=1, source_target_pairs={{0,15},{1,0},{2,1},{3,2},{4,3},{5,4},{6,5},{7,6},{8,7},{9,8},{10,9... | collective-permute-start | bytes 3080 | tf_op jit(solution)/shard_map/ppermute | solution.py:26
  82.0 1.2 collective-permute-done.12
  83.2 0.0 collective-permute-start.14
  83.2 0.0 collective-permute-done.13
  83.3 5.7 %collective-permute-done.14 = bf16[8,64]{1,0:T(8,128)(2,1)S(1)} collective-permute-done((bf16[8,64]{1,0:T(8,128)(2,1)S(1)}, bf16[8,64]{1,0:T(8,128)(2,1)S(1)}, u32[]{:S(2)}, u32[]{:S(2)}) %collective-permute-start.14) | collective-permute-done | bytes 1056 | tf_op jit(solution)/shard_map/ppermute | solution.py:21
  88.9 3.2 %multiply_reduce_fusion = f32[128]{0:T(128)S(1)} fusion(bf16[128,16384]{1,0:T(8,128)(2,1)} %all-gather.2.cloned.1.call-done), kind=kLoop, calls=%fused_computation | loop fusion | flops 6291328 | bytes 4194816 | tf_op jit(solution)/shard_map/reduce_sum | solution.py:34
  92.1 0.0 copy-done.1
  92.2 0.2 copy-done
  92.4 1.3 convert_reduce_fusion
  93.7 0.1 convolution_divide_fusion
  93.8 0.0 copy-done.2
  93.8 0.2 convolution_bitcast_fusion
  94.0 57.6 %psum.7 = f32[64,64]{0,1:T(8,128)S(1)} all-reduce(f32[64,64]{0,1:T(8,128)S(1)} %convolution_bitcast_fusion), channel_id=1, replica_groups=mesh['groups'=2,'blk'=16] {'blk'}, use_global_device_ids=true, to_apply=%region_3.4 | all-reduce | flops 4096 | bytes 32768 | tf_op jit(solution)/shard_map/psum | solution.py:62
  151.7 0.7 fusion.8
  152.4 0.7 copy.5
  (21 shorter events, 0.1 us)
Async XLA Ops:
  7.2 85.0 %copy-start.1 = (bf16[8,16384]{1,0:T(8,128)(2,1)S(1)}, bf16[8,16384]{1,0:T(8,128)(2,1)}, u32[]{:S(2)}) copy-start(bf16[8,16384]{1,0:T(8,128)(2,1)} %param.3) | copy-start | bytes 786436
  7.2 81.7 %all-gather.2.cloned.1.call-start = ((), (), s32[]{:S(2)}) async-start(), calls=%async_computation | async-start | bytes 4456448 | tf_op jit(solution)/shard_map/all_gather | solution.py:45
  7.9 40.9 %collective-permute-start = (bf16[8,64]{1,0:T(8,128)(2,1)}, bf16[8,64]{1,0:T(8,128)(2,1)S(1)}, u32[]{:S(2)}, u32[]{:S(2)}) collective-permute-start(bf16[8,64]{1,0:T(8,128)(2,1)} %param.4), channel_id=1, source_target_pairs={{0,1},{1,2},{2,3},{3,4},{4,5},{5,6},{6,7},{7,8},{8,9},{9,10},{10,1... | collective-permute-start | bytes 3080 | tf_op jit(solution)/shard_map/ppermute | solution.py:21
  8.4 40.4 %collective-permute-start.1 = (bf16[8,64]{1,0:T(8,128)(2,1)}, bf16[8,64]{1,0:T(8,128)(2,1)S(1)}, u32[]{:S(2)}, u32[]{:S(2)}) collective-permute-start(bf16[8,64]{1,0:T(8,128)(2,1)} %param.4), channel_id=1, source_target_pairs={{0,15},{1,0},{2,1},{3,2},{4,3},{5,4},{6,5},{7,6},{8,7},{9,8},{10,9... | collective-permute-start | bytes 3080 | tf_op jit(solution)/shard_map/ppermute | solution.py:26
  48.8 5.8 %collective-permute-start.2 = (bf16[8,64]{1,0:T(8,128)(2,1)S(1)}, bf16[8,64]{1,0:T(8,128)(2,1)S(1)}, u32[]{:S(2)}, u32[]{:S(2)}) collective-permute-start(bf16[8,64]{1,0:T(8,128)(2,1)S(1)} %collective-permute-done), channel_id=1, source_target_pairs={{0,1},{1,2},{2,3},{3,4},{4,5},{5,6},{6,7},{7,8},{8,9},{9,10},{10,1... | collective-permute-start | bytes 3080 | tf_op jit(solution)/shard_map/ppermute | solution.py:21
  48.8 5.7 %collective-permute-start.3 = (bf16[8,64]{1,0:T(8,128)(2,1)S(1)}, bf16[8,64]{1,0:T(8,128)(2,1)S(1)}, u32[]{:S(2)}, u32[]{:S(2)}) collective-permute-start(bf16[8,64]{1,0:T(8,128)(2,1)S(1)} %collective-permute-done.1), channel_id=1, source_target_pairs={{0,15},{1,0},{2,1},{3,2},{4,3},{5,4},{6,5},{7,6},{8,7},{9,8},{10,9... | collective-permute-start | bytes 3080 | tf_op jit(solution)/shard_map/ppermute | solution.py:26
  54.5 5.8 %collective-permute-start.4 = (bf16[8,64]{1,0:T(8,128)(2,1)S(1)}, bf16[8,64]{1,0:T(8,128)(2,1)S(1)}, u32[]{:S(2)}, u32[]{:S(2)}) collective-permute-start(bf16[8,64]{1,0:T(8,128)(2,1)S(1)} %collective-permute-done.2), channel_id=1, source_target_pairs={{0,1},{1,2},{2,3},{3,4},{4,5},{5,6},{6,7},{7,8},{8,9},{9,10},{10,1... | collective-permute-start | bytes 3080 | tf_op jit(solution)/shard_map/ppermute | solution.py:21
  54.6 5.8 %collective-permute-start.5 = (bf16[8,64]{1,0:T(8,128)(2,1)S(1)}, bf16[8,64]{1,0:T(8,128)(2,1)S(1)}, u32[]{:S(2)}, u32[]{:S(2)}) collective-permute-start(bf16[8,64]{1,0:T(8,128)(2,1)S(1)} %collective-permute-done.3), channel_id=1, source_target_pairs={{0,15},{1,0},{2,1},{3,2},{4,3},{5,4},{6,5},{7,6},{8,7},{9,8},{10,9... | collective-permute-start | bytes 3080 | tf_op jit(solution)/shard_map/ppermute | solution.py:26
  60.4 5.7 %collective-permute-start.6 = (bf16[8,64]{1,0:T(8,128)(2,1)S(1)}, bf16[8,64]{1,0:T(8,128)(2,1)S(1)}, u32[]{:S(2)}, u32[]{:S(2)}) collective-permute-start(bf16[8,64]{1,0:T(8,128)(2,1)S(1)} %collective-permute-done.4), channel_id=1, source_target_pairs={{0,1},{1,2},{2,3},{3,4},{4,5},{5,6},{6,7},{7,8},{8,9},{9,10},{10,1... | collective-permute-start | bytes 3080 | tf_op jit(solution)/shard_map/ppermute | solution.py:21
  60.4 5.7 %collective-permute-start.7 = (bf16[8,64]{1,0:T(8,128)(2,1)S(1)}, bf16[8,64]{1,0:T(8,128)(2,1)S(1)}, u32[]{:S(2)}, u32[]{:S(2)}) collective-permute-start(bf16[8,64]{1,0:T(8,128)(2,1)S(1)} %collective-permute-done.5), channel_id=1, source_target_pairs={{0,15},{1,0},{2,1},{3,2},{4,3},{5,4},{6,5},{7,6},{8,7},{9,8},{10,9... | collective-permute-start | bytes 3080 | tf_op jit(solution)/shard_map/ppermute | solution.py:26
  66.1 5.7 %collective-permute-start.8 = (bf16[8,64]{1,0:T(8,128)(2,1)S(1)}, bf16[8,64]{1,0:T(8,128)(2,1)S(1)}, u32[]{:S(2)}, u32[]{:S(2)}) collective-permute-start(bf16[8,64]{1,0:T(8,128)(2,1)S(1)} %collective-permute-done.6), channel_id=1, source_target_pairs={{0,1},{1,2},{2,3},{3,4},{4,5},{5,6},{6,7},{7,8},{8,9},{9,10},{10,1... | collective-permute-start | bytes 3080 | tf_op jit(solution)/shard_map/ppermute | solution.py:21
  66.1 5.7 %collective-permute-start.9 = (bf16[8,64]{1,0:T(8,128)(2,1)S(1)}, bf16[8,64]{1,0:T(8,128)(2,1)S(1)}, u32[]{:S(2)}, u32[]{:S(2)}) collective-permute-start(bf16[8,64]{1,0:T(8,128)(2,1)S(1)} %collective-permute-done.7), channel_id=1, source_target_pairs={{0,15},{1,0},{2,1},{3,2},{4,3},{5,4},{6,5},{7,6},{8,7},{9,8},{10,9... | collective-permute-start | bytes 3080 | tf_op jit(solution)/shard_map/ppermute | solution.py:26
  71.8 5.7 %collective-permute-start.10 = (bf16[8,64]{1,0:T(8,128)(2,1)S(1)}, bf16[8,64]{1,0:T(8,128)(2,1)S(1)}, u32[]{:S(2)}, u32[]{:S(2)}) collective-permute-start(bf16[8,64]{1,0:T(8,128)(2,1)S(1)} %collective-permute-done.8), channel_id=1, source_target_pairs={{0,1},{1,2},{2,3},{3,4},{4,5},{5,6},{6,7},{7,8},{8,9},{9,10},{10,1... | collective-permute-start | bytes 3080 | tf_op jit(solution)/shard_map/ppermute | solution.py:21
  71.8 5.7 %collective-permute-start.11 = (bf16[8,64]{1,0:T(8,128)(2,1)S(1)}, bf16[8,64]{1,0:T(8,128)(2,1)S(1)}, u32[]{:S(2)}, u32[]{:S(2)}) collective-permute-start(bf16[8,64]{1,0:T(8,128)(2,1)S(1)} %collective-permute-done.9), channel_id=1, source_target_pairs={{0,15},{1,0},{2,1},{3,2},{4,3},{5,4},{6,5},{7,6},{8,7},{9,8},{10,9... | collective-permute-start | bytes 3080 | tf_op jit(solution)/shard_map/ppermute | solution.py:26
  77.5 5.7 %collective-permute-start.12 = (bf16[8,64]{1,0:T(8,128)(2,1)S(1)}, bf16[8,64]{1,0:T(8,128)(2,1)S(1)}, u32[]{:S(2)}, u32[]{:S(2)}) collective-permute-start(bf16[8,64]{1,0:T(8,128)(2,1)S(1)} %collective-permute-done.10), channel_id=1, source_target_pairs={{0,1},{1,2},{2,3},{3,4},{4,5},{5,6},{6,7},{7,8},{8,9},{9,10},{10,1... | collective-permute-start | bytes 3080 | tf_op jit(solution)/shard_map/ppermute | solution.py:21
  77.5 5.7 %collective-permute-start.13 = (bf16[8,64]{1,0:T(8,128)(2,1)S(1)}, bf16[8,64]{1,0:T(8,128)(2,1)S(1)}, u32[]{:S(2)}, u32[]{:S(2)}) collective-permute-start(bf16[8,64]{1,0:T(8,128)(2,1)S(1)} %collective-permute-done.11), channel_id=1, source_target_pairs={{0,15},{1,0},{2,1},{3,2},{4,3},{5,4},{6,5},{7,6},{8,7},{9,8},{10,9... | collective-permute-start | bytes 3080 | tf_op jit(solution)/shard_map/ppermute | solution.py:26
  83.2 5.7 %collective-permute-start.14 = (bf16[8,64]{1,0:T(8,128)(2,1)S(1)}, bf16[8,64]{1,0:T(8,128)(2,1)S(1)}, u32[]{:S(2)}, u32[]{:S(2)}) collective-permute-start(bf16[8,64]{1,0:T(8,128)(2,1)S(1)} %collective-permute-done.12), channel_id=1, source_target_pairs={{0,1},{1,2},{2,3},{3,4},{4,5},{5,6},{6,7},{7,8},{8,9},{9,10},{10,1... | collective-permute-start | bytes 3080 | tf_op jit(solution)/shard_map/ppermute | solution.py:21
  88.9 3.5 %copy-start = (bf16[128,16384]{1,0:T(8,128)(2,1)S(1)}, bf16[128,16384]{1,0:T(8,128)(2,1)}, u32[]{:S(2)}) copy-start(bf16[128,16384]{1,0:T(8,128)(2,1)} %all-gather.2.cloned.1.call-done) | copy-start | bytes 12582916
  88.9 4.9 %copy-start.2 = (bf16[8,64]{1,0:T(8,128)(2,1)S(1)}, bf16[8,64]{1,0:T(8,128)(2,1)}, u32[]{:S(2)}) copy-start(bf16[8,64]{1,0:T(8,128)(2,1)} %param.4) | copy-start | bytes 3076
Sparse Core Ops, SparseCore 0:
  10.2 53.5 all-gather.1
